TPU v7x, 32 devices: a whole 2x2x4 slice. The times are simulated.
32 devices in a mesh: groups: 2 (over x), src: 8 (over z, y), tile: 2 (over core).
Axes of the slice: x: 2, y: 2, z: 4, core: 2. Of those that a mesh axis runs over, the one named last changes fastest.
Arguments:
- mask: float32 [2048, 1024], P(('groups', 'tile')), parts along dimension 0, may hold values from 0 to 1
- target: float32 [2048, 1024], P(('groups', 'tile')), parts along dimension 0, may hold values from 0 to 1
- pupil: float32 [64, 64], replicated, may hold values from 0.1 to 1.9
- source_shift: int32 [24, 2], replicated, may hold values from -24 to 24
- source_weight: float32 [24], replicated, may hold values from 0.25 to 4
Outputs:
- mask_gradient: float32 [2048, 1024], P(('groups', 'tile'), 'src'), parts along dimension 0
There are 2 independent parts, one for each index of `groups`. A program takes and returns all parts, laid end to end along the dimension named above; an argument that names none is the same for every part. Nothing has to cross between parts.
Inputs may be any that keep to these rules, and one draw needn't show every extreme that they name: `source_shift`: integer frequency shifts of the source points.
All inputs are finite; a program needn't handle non-finite values.
Results may differ from a plain program's by a relative error of at most 0.0003.
Values sent between devices are 32-bit elements; how exact they have to be, the bound alone decides.
A program may use at most 128 MiB of HBM per device.

v0:
```python
import numpy as np
import jax
import jax.numpy as jnp
from jax import lax
from jax.sharding import PartitionSpec as P

TS = 512
HALO = 64
PAD = 640
GRID = 128
REACH = 24
exact_mode = lax.Precision.HIGHEST
resist_gain = 25.0
resist_level = 0.25


def tables(freqs, columns):
    pixels = np.arange(PAD)[:, None]
    samples = np.arange(GRID)[None, :] * (PAD // GRID)
    spread = np.ones((PAD, GRID))
    for p in range(1, GRID // 2):
        spread += 2.0 * np.cos(2.0 * np.pi * (p * (pixels - samples) % PAD) / PAD)
    spread /= GRID
    tiles = columns // TS
    across = np.zeros((columns, tiles * GRID))
    for c in range(tiles):
        low, high = (max(0, c * TS - HALO), min(columns, c * TS - HALO + PAD))
        across[low:high, c * GRID : (c + 1) * GRID] = spread[
            low + HALO - c * TS : high + HALO - c * TS
        ]
    bins = np.arange(-freqs // 2 - REACH, freqs // 2 + REACH)[:, None] * np.arange(GRID)[None, :]
    angle = 2.0 * np.pi * (bins % GRID) / GRID
    waves = np.concatenate([np.cos(angle), np.sin(angle)], axis=1)
    return (spread, across, waves)


def rotation(waves, freqs):
    centre = waves[REACH : REACH + freqs]
    cosine, sine = (centre[:, :GRID].T, centre[:, GRID:].T)
    return np.block([[cosine, -sine], [sine, cosine]])


def mm(a, b):
    return jnp.dot(a, b, precision=exact_mode, preferred_element_type=jnp.float32)


def resist_slope(intensity, target):
    printed = jax.nn.sigmoid(resist_gain * (intensity - resist_level))
    return 2.0 * (printed - target) * resist_gain * printed * (1.0 - printed)


def halves(y, tiles, freqs):
    real, imag = ([], [])
    for c in range(tiles):
        top = y[2 * c * freqs : (2 * c + 1) * freqs]
        low = y[(2 * c + 1) * freqs : (2 * c + 2) * freqs]
        real.append(top[:, :GRID] - low[:, GRID:])
        imag.append(top[:, GRID:] + low[:, :GRID])
    return (jnp.concatenate(real, axis=1), jnp.concatenate(imag, axis=1))


def shards(mask, target, pupil, source_shift, source_weight):
    f32 = jnp.float32
    me = lax.axis_index("src")
    n = lax.axis_size("src")
    nt = lax.axis_size("tile")
    own = source_shift.shape[0] // n
    freqs = pupil.shape[0]
    columns = mask.shape[1]
    tiles = columns // TS
    width = columns // n
    spread64, across64, waves64 = tables(freqs, columns)
    spread = jnp.asarray(spread64, f32)
    core = spread[HALO : HALO + TS]
    across = jnp.asarray(across64, f32)
    waves = jnp.asarray(waves64, f32)
    fixed = jnp.asarray(waves64[REACH : REACH + freqs], f32)
    turn = jnp.asarray(rotation(waves64, freqs), f32)
    total = jnp.sum(source_weight)
    scaled = jnp.tile(pupil / (PAD * PAD), (2 * tiles, 1))
    above = lax.ppermute(mask[TS - HALO :], "tile", [(i, i + 1) for i in range(nt - 1)])
    below = lax.ppermute(mask[:HALO], "tile", [(i + 1, i) for i in range(nt - 1)])
    strip = jnp.concatenate([above, mask, below], axis=0)
    low = mm(mm(spread.T, strip), across)
    zc = mm(waves[:, :GRID], low)
    zs = mm(waves[:, GRID:], low)
    fields = []
    light = jnp.zeros((GRID, tiles * GRID), f32)
    for s in range(own):
        a = source_shift[me * own + s, 0] + REACH
        b = source_shift[me * own + s, 1] + REACH
        w = source_weight[me * own + s]
        c_rows = lax.dynamic_slice_in_dim(zc, a, freqs, 0)
        s_rows = lax.dynamic_slice_in_dim(zs, a, freqs, 0)
        shifted = lax.dynamic_slice_in_dim(waves, b, freqs, 0)
        rows = []
        for c in range(tiles):
            cc = c_rows[:, c * GRID : (c + 1) * GRID]
            ss = s_rows[:, c * GRID : (c + 1) * GRID]
            rows.append(jnp.concatenate([cc, -ss], axis=1))
            rows.append(jnp.concatenate([-ss, -cc], axis=1))
        spec = mm(jnp.concatenate(rows, axis=0), shifted.T) * scaled
        real, imag = halves(mm(spec, fixed), tiles, freqs)
        field = mm(turn, jnp.concatenate([real, imag], axis=0))
        fields.append(field)
        light = light + w * (field[:GRID] * field[:GRID] + field[GRID:] * field[GRID:])
    light = lax.psum(light, "src")
    up = mm(core, light)
    backs = []
    for c in range(tiles):
        fine = mm(up[:, c * GRID : (c + 1) * GRID], core.T)
        slope = resist_slope(fine / total, target[:, c * TS : (c + 1) * TS]) / total
        backs.append(mm(slope, core))
    pull = mm(core.T, jnp.concatenate(backs, axis=1))
    pull = jnp.concatenate([pull, pull], axis=0)
    grid_grad = jnp.zeros((GRID, tiles * GRID), f32)
    for s in range(own):
        a = source_shift[me * own + s, 0] + REACH
        b = source_shift[me * own + s, 1] + REACH
        w = source_weight[me * own + s]
        shift_a = lax.dynamic_slice_in_dim(waves, a, freqs, 0)
        shift_b = lax.dynamic_slice_in_dim(waves, b, freqs, 0)
        u = mm(turn.T, fields[s] * pull * (2.0 * w))
        rows = []
        for c in range(tiles):
            re = u[:freqs, c * GRID : (c + 1) * GRID]
            im = u[freqs:, c * GRID : (c + 1) * GRID]
            rows.append(jnp.concatenate([re, im], axis=1))
            rows.append(jnp.concatenate([im, -re], axis=1))
        back = mm(jnp.concatenate(rows, axis=0), fixed.T) * scaled
        real, imag = halves(mm(back, shift_b), tiles, freqs)
        grid_grad = grid_grad + mm(shift_a[:, :GRID].T, real) - mm(shift_a[:, GRID:].T, imag)
    grid_grad = lax.psum(grid_grad, "src")
    cols = lax.dynamic_slice_in_dim(across, me * width, width, 0)
    full = mm(spread, mm(grid_grad, cols.T))
    upper, inner, lower = (full[:HALO], full[HALO : HALO + TS], full[HALO + TS :])
    from_above = lax.ppermute(lower, "tile", [(i, i + 1) for i in range(nt - 1)])
    from_below = lax.ppermute(upper, "tile", [(i + 1, i) for i in range(nt - 1)])
    inner = inner.at[:HALO].add(from_above)
    return inner.at[TS - HALO :].add(from_below)


def solution(mesh):
    placed = (P(("groups", "tile"), None), P(("groups", "tile"), None), P(), P(), P())
    return jax.shard_map(
        shards, mesh=mesh, in_specs=placed, out_specs=P(("groups", "tile"), "src"), check_vma=False
    )
```

profile of v0, /device:TPU:0, one launch (start us, length us, event | category | flops | bytes accessed | tf_op | source)
XLA Modules:
  0.0 207.0 jit_solution(10192906300589848366)
XLA Ops:
  6.5 0.0 all-reduce.3.cloned.1.call-start
  6.6 1.1 fusion.238
  7.7 0.0 copy-start.11
  7.7 1.3 collective-permute-start.1
  9.0 3.1 %collective-permute-start = (f32[64,1024]{1,0:T(8,128)S(1)}, f32[64,1024]{1,0:T(8,128)S(1)}, u32[]{:S(2)}, u32[]{:S(2)}) collective-permute-start(f32[64,1024]{1,0:T(8,128)S(1)} %get-tuple-element.29), channel_id=1, source_target_pairs={{0,1},{2,3},{4,5},{6,7},{8,9},{10,11},{12,13},{14,15},{16,17},{18,... | collective-permute-start | bytes 786440 | tf_op jit(solution)/shard_map/ppermute | solution.py:81
  12.0 3.0 %fusion.247 = f32[128,1024]{1,0:T(8,128)S(1)} fusion(f32[512,128]{1,0:T(8,128)} %constant.135, f32[512,1024]{1,0:T(8,128)} %param.14), kind=kOutput, calls=%fused_computation.327 | convolution fusion | flops 805306368 | bytes 2883584 | tf_op jit(solution)/shard_map/dot_general | solution.py:44
  15.0 0.0 copy-start.2
  15.1 0.7 constant_dynamic-slice_fusion.4
  23.1 0.7 fusion.246
  23.8 0.6 fusion.248
  24.4 0.0 copy-start.9
  24.5 0.7 fusion.10
  25.1 0.0 copy-start.1
  25.2 0.0 copy-start.6
  25.2 0.6 fusion.249
  25.8 0.3 fusion.250
  26.1 0.3 fusion.251
  26.5 0.4 convolution_multiply_fusion.4
  26.9 0.3 fusion.253
  27.3 0.0 copy-start.3
  27.3 0.4 convolution_multiply_fusion.3
  27.7 0.3 fusion.254
  28.1 0.4 convolution_multiply_fusion.5
  28.5 0.3 fusion.252
  28.9 0.4 fusion.161
  29.3 0.4 fusion.168
  29.7 0.4 fusion.154
  30.2 0.4 fusion.12
  30.6 0.4 fusion.11
  31.0 0.4 fusion.13
  31.4 2.4 %fusion.134 = f32[128,256]{0,1:T(8,128)} fusion(f32[256,256]{0,1:T(8,128)S(1)} %fusion.11, f32[256,256]{0,1:T(8,128)S(1)} %fusion.12, f32[256,256]{0,1:T(8,128)S(1)} %fusion.13, f32[]{:T(128)} %bitcast.17, f32[]{:T(128)} %bitcast.9, f32[]{:T(128)} %bitcast.8), kind=kLoop, calls=%fused_computation.152 | loop fusion | flops 458752 | bytes 917516 | tf_op jit(solution)/shard_map/add | solution.py:106
  33.9 0.0 all-reduce.3.cloned.1.call-update
  33.9 0.2 all-reduce.5.cloned.1.call-start
  35.9 0.6 reduce_sum.9
  36.4 70.7 %all-reduce.3.cloned.1.call-done = f32[128,256]{0,1:T(8,128)} async-done(((f32[128,256]{0,1:T(8,128)}), f32[128,256]{0,1:T(8,128)}) %all-reduce.3.cloned.1.call-update) | async-done | bytes 131088 | tf_op jit(solution)/shard_map/psum | solution.py:107
  107.2 1.5 fusion.255
  108.7 1.7 fusion.15
  110.4 1.9 fusion.14
  112.3 1.6 fusion.16
  114.0 1.7 fusion.17
  115.6 1.0 fusion.18
  116.6 0.4 fusion.85
  117.1 0.4 convolution_multiply_fusion
  117.4 0.4 fusion.145
  117.8 0.4 fusion.82
  118.3 0.4 convolution_multiply_fusion.1
  118.6 0.4 fusion.148
  119.0 0.4 fusion.79
  119.5 0.4 convolution_multiply_fusion.2
  119.8 0.4 fusion.151
  120.2 0.3 fusion.175
  120.6 0.4 convolution_subtract_fusion.2
  121.0 0.3 convolution_add_fusion.5
  121.3 0.4 convolution_subtract_fusion.1
  121.7 0.3 convolution_add_fusion.4
  122.0 1.0 convolution_subtract_fusion
  123.1 0.0 all-reduce.5.cloned.1.call-update
  123.1 69.6 %all-reduce.5.cloned.1.call-done = f32[128,256]{1,0:T(8,128)} async-done(((f32[128,256]{1,0:T(8,128)}), f32[128,256]{1,0:T(8,128)}) %all-reduce.5.cloned.1.call-update) | async-done | bytes 131088 | tf_op jit(solution)/shard_map/psum | solution.py:133
  192.7 1.2 fusion.140
  193.9 0.4 fusion.256
  194.4 1.3 collective-permute-start.2
  195.7 1.3 collective-permute-start.3
  197.0 1.8 collective-permute-done.3
  198.8 1.4 fusion.194
  (52 shorter events, 0.4 us)
Async XLA Ops:
  6.5 17.3 %copy-start.12 = (f32[64,128]{1,0:T(8,128)S(1)}, f32[64,128]{1,0:T(8,128)}, u32[]{:S(2)}) copy-start(f32[64,128]{1,0:T(8,128)} %constant.136) | copy-start | bytes 98308
  6.5 8.5 %copy-start.13 = (f32[64,64]{1,0:T(8,128)S(1)}, f32[64,64]{1,0:T(8,128)}, u32[]{:S(2)}) copy-start(f32[64,64]{1,0:T(8,128)} %param.16) | copy-start | bytes 49156
  6.5 8.5 %copy-start.14 = (s32[24,2]{0,1:T(2,128)S(1)}, s32[24,2]{0,1:T(2,128)}, u32[]{:S(2)}) copy-start(s32[24,2]{0,1:T(2,128)} %param.17) | copy-start | bytes 580
  6.5 16.6 %copy-start.15 = (f32[24]{0:T(128)S(1)}, f32[24]{0:T(128)}, u32[]{:S(2)}) copy-start(f32[24]{0:T(128)} %param.18) | copy-start | bytes 292
  6.5 100.6 %all-reduce.3.cloned.1.call-start = ((), (), s32[]{:S(2)}) async-start(), calls=%async_computation | async-start | bytes 262144 | tf_op jit(solution)/shard_map/psum | solution.py:107
  7.7 16.8 %copy-start.11 = (f32[64,128]{1,0:T(8,128)S(1)}, f32[64,128]{1,0:T(8,128)}, u32[]{:S(2)}) copy-start(f32[64,128]{1,0:T(8,128)} %constant.134) | copy-start | bytes 98308
  7.7 16.1 %collective-permute-start.1 = (f32[64,1024]{1,0:T(8,128)S(1)}, f32[64,1024]{1,0:T(8,128)S(1)}, u32[]{:S(2)}, u32[]{:S(2)}) collective-permute-start(f32[64,1024]{1,0:T(8,128)S(1)} %get-tuple-element.30), channel_id=1, source_target_pairs={{1,0},{3,2},{5,4},{7,6},{9,8},{11,10},{13,12},{15,14},{17,16},{19,... | collective-permute-start | bytes 786440 | tf_op jit(solution)/shard_map/ppermute | solution.py:82
  9.0 15.5 %collective-permute-start = (f32[64,1024]{1,0:T(8,128)S(1)}, f32[64,1024]{1,0:T(8,128)S(1)}, u32[]{:S(2)}, u32[]{:S(2)}) collective-permute-start(f32[64,1024]{1,0:T(8,128)S(1)} %get-tuple-element.29), channel_id=1, source_target_pairs={{0,1},{2,3},{4,5},{6,7},{8,9},{10,11},{12,13},{14,15},{16,17},{18,... | collective-permute-start | bytes 786440 | tf_op jit(solution)/shard_map/ppermute | solution.py:81
  15.0 10.1 %copy-start.2 = (f32[1024,256]{1,0:T(8,128)S(1)}, f32[1024,256]{1,0:T(8,128)}, u32[]{:S(2)}) copy-start(f32[1024,256]{1,0:T(8,128)} %constant.130.clone) | copy-start | bytes 3145732
  23.8 2.0 copy-start.10
  24.4 1.7 copy-start.9
  25.1 1.3 copy-start.1
  25.2 1.7 copy-start.6
  27.3 1.6 copy-start.3
  28.0 2.1 %copy-start.5 = (f32[256,64]{1,0:T(8,128)S(1)}, f32[256,64]{1,0:T(8,128)}, u32[]{:S(2)}) copy-start(f32[256,64]{1,0:T(8,128)} %constant.140) | copy-start | bytes 196612
  29.3 77.9 %copy-start = (f32[512,128]{1,0:T(8,128)S(1)}, f32[512,128]{1,0:T(8,128)}, u32[]{:S(2)}) copy-start(f32[512,128]{1,0:T(8,128)} %constant.135) | copy-start | bytes 786436
  33.9 158.8 %all-reduce.5.cloned.1.call-start = ((), (), s32[]{:S(2)}) async-start(), calls=%async_computation.1 | async-start | bytes 262144 | tf_op jit(solution)/shard_map/psum | solution.py:133
  110.4 1.9 copy-start.16
  113.9 2.7 %copy-start.4 = (f32[256,128]{1,0:T(8,128)S(1)}, f32[256,128]{1,0:T(8,128)}, u32[]{:S(2)}) copy-start(f32[256,128]{1,0:T(8,128)} %constant.133.clone) | copy-start | bytes 393220
  119.5 74.5 %copy-start.8 = (f32[640,128]{1,0:T(8,128)S(1)}, f32[640,128]{1,0:T(8,128)}, u32[]{:S(2)}) copy-start(f32[640,128]{1,0:T(8,128)} %constant.129.clone) | copy-start | bytes 983044
  194.4 2.6 %collective-permute-start.2 = (f32[64,128]{1,0:T(8,128)S(1)}, f32[64,128]{1,0:T(8,128)S(1)}, u32[]{:S(2)}, u32[]{:S(2)}) collective-permute-start(f32[64,128]{1,0:T(8,128)S(1)} %get-tuple-element.32), channel_id=1, source_target_pairs={{0,1},{2,3},{4,5},{6,7},{8,9},{10,11},{12,13},{14,15},{16,17},{18,... | collective-permute-start | bytes 98312 | tf_op jit(solution)/shard_map/ppermute | solution.py:137
  195.7 3.1 %collective-permute-start.3 = (f32[64,128]{1,0:T(8,128)S(1)}, f32[64,128]{1,0:T(8,128)S(1)}, u32[]{:S(2)}, u32[]{:S(2)}) collective-permute-start(f32[64,128]{1,0:T(8,128)S(1)} %get-tuple-element.31), channel_id=1, source_target_pairs={{1,0},{3,2},{5,4},{7,6},{9,8},{11,10},{13,12},{15,14},{17,16},{19,... | collective-permute-start | bytes 98312 | tf_op jit(solution)/shard_map/ppermute | solution.py:138
  197.0 1.8 copy-start.7
Sparse Core Ops, SparseCore 0:
  34.0 73.0 all-reduce.2
  123.2 69.4 all-reduce.4
where the time goes:
time: 208 us; the launch traced here: 207 us
  waiting for transfers between devices  142 us (68%)
  matrix products  27.2 us (13%)
  between operations  23.3 us (11%)
  starting transfers between devices  7.19 us (3%)
  other arithmetic  4.61 us (2%)
  local copies, waits for them, and re-layouts  2.58 us (1%)
    psum x1, waiting for transfers between devices, shards(): light = lax.psum(light, 'src')  70.7 us
    psum x1, waiting for transfers between devices, shards(): grid_grad = lax.psum(grid_grad, 'src')  69.6 us
    dot_general x41, matrix products, mm(): jnp.dot(a, b, precision=exact_mode, preferred_element_type=jnp.float32)  27.2 us
  transfers between devices with their start and end apart: 6, of which 3 were waited for; matrix products, arithmetic and copies ran while one was open for 3% of the time, Pallas kernels for 0%

commit v1 on v0

--- a/solution.py
+++ b/solution.py
@@ -104,7 +104,8 @@
         field = mm(turn, jnp.concatenate([real, imag], axis=0))
         fields.append(field)
         light = light + w * (field[:GRID] * field[:GRID] + field[GRID:] * field[GRID:])
-    light = lax.psum(light, "src")
+    carry = lax.all_gather(light, "src")
+    light = jnp.sum(carry, 0)
     up = mm(core, light)
     backs = []
     for c in range(tiles):

time: 208 us -> 178 us (0.86)
  waiting for transfers between devices: 142 us -> 111 us
    psum x1 -> x0, waiting for transfers between devices: 70.7 us -> none  [shards(): light = lax.psum(light, 'src')]
    all_gather x0 -> x1, waiting for transfers between devices: none -> 39.4 us  [shards(): carry = lax.all_gather(light, 'src')]
where the time goes in v1:
time: 178 us; the launch traced here: 177 us
  waiting for transfers between devices  111 us (62%)
  matrix products  26.6 us (15%)
  between operations  23.5 us (13%)
  starting transfers between devices  7.19 us (4%)
  other arithmetic  5.22 us (3%)
  local copies, waits for them, and re-layouts  4.01 us (2%)
    psum x1, waiting for transfers between devices, shards(): grid_grad = lax.psum(grid_grad, 'src')  69.6 us
    all_gather x1, waiting for transfers between devices, shards(): carry = lax.all_gather(light, 'src')  39.4 us
    dot_general x41, matrix products, mm(): jnp.dot(a, b, precision=exact_mode, preferred_element_type=jnp.float32)  26.6 us
  transfers between devices with their start and end apart: 6, of which 3 were waited for; matrix products, arithmetic and copies ran while one was open for 3% of the time, Pallas kernels for 0%

profile of v1, /device:TPU:0, one launch (start us, length us, event | category | flops | bytes accessed | tf_op | source)
XLA Modules:
  0.0 177.4 jit_solution(7165869082882650602)
XLA Ops:
  6.5 0.0 all-gather.3.cloned.1.call-start
  6.6 1.1 fusion.238
  7.7 0.0 copy-start.11
  7.7 1.3 collective-permute-start.1
  9.0 3.1 %collective-permute-start = (f32[64,1024]{1,0:T(8,128)S(1)}, f32[64,1024]{1,0:T(8,128)S(1)}, u32[]{:S(2)}, u32[]{:S(2)}) collective-permute-start(f32[64,1024]{1,0:T(8,128)S(1)} %get-tuple-element.29), channel_id=1, source_target_pairs={{0,1},{2,3},{4,5},{6,7},{8,9},{10,11},{12,13},{14,15},{16,17},{18,... | collective-permute-start | bytes 786440 | tf_op jit(solution)/shard_map/ppermute | solution.py:81
  12.0 3.0 %fusion.247 = f32[128,1024]{1,0:T(8,128)S(1)} fusion(f32[512,128]{1,0:T(8,128)} %constant.135, f32[512,1024]{1,0:T(8,128)} %param.14), kind=kOutput, calls=%fused_computation.328 | convolution fusion | flops 805306368 | bytes 2883584 | tf_op jit(solution)/shard_map/dot_general | solution.py:44
  15.0 0.0 copy-start.2
  15.1 0.7 constant_dynamic-slice_fusion.4
  23.1 0.7 fusion.246
  23.8 0.6 fusion.248
  24.4 0.0 copy-start.9
  24.5 0.7 fusion.10
  25.2 0.0 copy-start.6
  25.2 0.6 fusion.249
  25.8 0.3 fusion.250
  26.1 0.3 fusion.251
  26.5 0.4 convolution_multiply_fusion.4
  26.9 0.3 fusion.253
  27.3 0.4 convolution_multiply_fusion.3
  27.7 0.3 fusion.254
  28.1 0.4 convolution_multiply_fusion.5
  28.5 0.3 fusion.252
  28.9 0.4 fusion.161
  29.3 0.4 fusion.168
  29.7 0.4 fusion.154
  30.2 0.4 fusion.12
  30.6 0.4 fusion.11
  31.0 0.4 fusion.13
  31.5 2.7 %fusion.134 = f32[128,256]{0,1:T(8,128)} fusion(f32[256,256]{0,1:T(8,128)S(1)} %fusion.11, f32[256,256]{0,1:T(8,128)S(1)} %fusion.12, f32[256,256]{0,1:T(8,128)S(1)} %fusion.13, f32[]{:T(128)} %bitcast.17, f32[]{:T(128)} %bitcast.9, f32[]{:T(128)} %bitcast.8), kind=kLoop, calls=%fused_computation.153 | loop fusion | flops 458752 | bytes 917516 | tf_op jit(solution)/shard_map/add | solution.py:106
  34.2 0.0 all-gather.3.cloned.1.call-update
  34.2 0.2 all-reduce.2.cloned.1.call-start
  36.3 0.7 reduce_sum.19
  37.0 39.4 %all-gather.3.cloned.1.call-done = f32[1024,256]{0,1:T(8,128)} async-done(((f32[128,256]{0,1:T(8,128)}), f32[1024,256]{0,1:T(8,128)}) %all-gather.3.cloned.1.call-update) | async-done | bytes 1048592 | tf_op jit(solution)/shard_map/all_gather | solution.py:107
  76.4 1.4 copy.16
  77.9 0.3 bitcast_reduce_fusion
  78.1 0.6 fusion.255
  78.7 1.8 %fusion.15 = f32[512,512]{1,0:T(8,128)S(1)} fusion(f32[512,128]{1,0:T(8,128)S(1)} %copy-done, f32[]{:T(128)} %reduce_sum.19, f32[512,256]{1,0:T(8,128)S(1)} %fusion.255), kind=kOutput, calls=%fused_computation.21 | convolution fusion | flops 404226048 | bytes 1572868 | tf_op jit(solution)/shard_map/dot_general | solution.py:44
  80.6 2.0 %fusion.14 = f32[512,512]{1,0:T(8,128)S(1)} fusion(f32[512,128]{1,0:T(8,128)S(1)} %copy-done, f32[]{:T(128)} %reduce_sum.19, f32[512,256]{1,0:T(8,128)S(1)} %fusion.255), kind=kOutput, calls=%fused_computation.20 | convolution fusion | flops 404226048 | bytes 1572868 | tf_op jit(solution)/shard_map/dot_general | solution.py:44
  82.5 1.7 fusion.16
  84.3 1.8 fusion.17
  86.0 1.0 fusion.18
  87.1 0.4 fusion.85
  87.5 0.4 convolution_multiply_fusion
  87.9 0.4 fusion.145
  88.2 0.4 fusion.82
  88.7 0.4 convolution_multiply_fusion.1
  89.0 0.4 fusion.148
  89.4 0.4 fusion.79
  89.9 0.4 convolution_multiply_fusion.2
  90.3 0.4 fusion.151
  90.6 0.3 fusion.175
  91.0 0.4 convolution_subtract_fusion.2
  91.4 0.3 convolution_add_fusion.5
  91.7 0.4 convolution_subtract_fusion.1
  92.1 0.3 convolution_add_fusion.4
  92.4 1.1 convolution_subtract_fusion
  93.5 0.0 all-reduce.2.cloned.1.call-update
  93.5 69.6 %all-reduce.2.cloned.1.call-done = f32[128,256]{1,0:T(8,128)} async-done(((f32[128,256]{1,0:T(8,128)}), f32[128,256]{1,0:T(8,128)}) %all-reduce.2.cloned.1.call-update) | async-done | bytes 131088 | tf_op jit(solution)/shard_map/psum | solution.py:134
  163.1 1.2 fusion.140
  164.3 0.4 fusion.256
  164.7 1.3 collective-permute-start.2
  166.1 1.3 collective-permute-start.3
  167.4 1.8 collective-permute-done.3
  169.2 1.4 fusion.194
  (54 shorter events, 0.4 us)
Async XLA Ops:
  6.5 17.3 %copy-start.12 = (f32[64,128]{1,0:T(8,128)S(1)}, f32[64,128]{1,0:T(8,128)}, u32[]{:S(2)}) copy-start(f32[64,128]{1,0:T(8,128)} %constant.136) | copy-start | bytes 98308
  6.5 8.5 %copy-start.13 = (f32[64,64]{1,0:T(8,128)S(1)}, f32[64,64]{1,0:T(8,128)}, u32[]{:S(2)}) copy-start(f32[64,64]{1,0:T(8,128)} %param.16) | copy-start | bytes 49156
  6.5 8.5 %copy-start.14 = (s32[24,2]{0,1:T(2,128)S(1)}, s32[24,2]{0,1:T(2,128)}, u32[]{:S(2)}) copy-start(s32[24,2]{0,1:T(2,128)} %param.17) | copy-start | bytes 580
  6.5 16.6 %copy-start.15 = (f32[24]{0:T(128)S(1)}, f32[24]{0:T(128)}, u32[]{:S(2)}) copy-start(f32[24]{0:T(128)} %param.18) | copy-start | bytes 292
  6.5 69.9 %all-gather.3.cloned.1.call-start = ((), (), s32[]{:S(2)}) async-start(), calls=%async_computation.1 | async-start | bytes 1179648 | tf_op jit(solution)/shard_map/all_gather | solution.py:107
  7.7 16.8 %copy-start.11 = (f32[64,128]{1,0:T(8,128)S(1)}, f32[64,128]{1,0:T(8,128)}, u32[]{:S(2)}) copy-start(f32[64,128]{1,0:T(8,128)} %constant.134) | copy-start | bytes 98308
  7.7 16.1 %collective-permute-start.1 = (f32[64,1024]{1,0:T(8,128)S(1)}, f32[64,1024]{1,0:T(8,128)S(1)}, u32[]{:S(2)}, u32[]{:S(2)}) collective-permute-start(f32[64,1024]{1,0:T(8,128)S(1)} %get-tuple-element.30), channel_id=1, source_target_pairs={{1,0},{3,2},{5,4},{7,6},{9,8},{11,10},{13,12},{15,14},{17,16},{19,... | collective-permute-start | bytes 786440 | tf_op jit(solution)/shard_map/ppermute | solution.py:82
  9.0 15.5 %collective-permute-start = (f32[64,1024]{1,0:T(8,128)S(1)}, f32[64,1024]{1,0:T(8,128)S(1)}, u32[]{:S(2)}, u32[]{:S(2)}) collective-permute-start(f32[64,1024]{1,0:T(8,128)S(1)} %get-tuple-element.29), channel_id=1, source_target_pairs={{0,1},{2,3},{4,5},{6,7},{8,9},{10,11},{12,13},{14,15},{16,17},{18,... | collective-permute-start | bytes 786440 | tf_op jit(solution)/shard_map/ppermute | solution.py:81
  15.0 10.1 %copy-start.2 = (f32[1024,256]{1,0:T(8,128)S(1)}, f32[1024,256]{1,0:T(8,128)}, u32[]{:S(2)}) copy-start(f32[1024,256]{1,0:T(8,128)} %constant.130.clone) | copy-start | bytes 3145732
  23.8 2.0 %copy-start.10 = (f32[112,128]{1,0:T(8,128)S(1)}, f32[112,128]{1,0:T(8,128)}, u32[]{:S(2)}) copy-start(f32[112,128]{1,0:T(8,128)} %constant.137) | copy-start | bytes 172036
  24.4 1.7 copy-start.9
  25.2 1.3 copy-start.1
  25.2 1.7 copy-start.6
  27.3 1.6 copy-start.3
  28.0 2.1 %copy-start.5 = (f32[256,64]{1,0:T(8,128)S(1)}, f32[256,64]{1,0:T(8,128)}, u32[]{:S(2)}) copy-start(f32[256,64]{1,0:T(8,128)} %constant.140) | copy-start | bytes 196612
  31.4 46.7 %copy-start = (f32[512,128]{1,0:T(8,128)S(1)}, f32[512,128]{1,0:T(8,128)}, u32[]{:S(2)}) copy-start(f32[512,128]{1,0:T(8,128)} %constant.135) | copy-start | bytes 786436
  34.2 128.9 %all-reduce.2.cloned.1.call-start = ((), (), s32[]{:S(2)}) async-start(), calls=%async_computation | async-start | bytes 262144 | tf_op jit(solution)/shard_map/psum | solution.py:134
  80.5 2.0 %copy-start.16 = (f32[512,1024]{1,0:T(8,128)S(1)}, f32[512,1024]{1,0:T(8,128)}, u32[]{:S(2)}) copy-start(f32[512,1024]{1,0:T(8,128)} %param.15) | copy-start | bytes 6291460
  84.3 2.8 %copy-start.4 = (f32[256,128]{1,0:T(8,128)S(1)}, f32[256,128]{1,0:T(8,128)}, u32[]{:S(2)}) copy-start(f32[256,128]{1,0:T(8,128)} %constant.133.clone) | copy-start | bytes 393220
  89.9 74.4 %copy-start.8 = (f32[640,128]{1,0:T(8,128)S(1)}, f32[640,128]{1,0:T(8,128)}, u32[]{:S(2)}) copy-start(f32[640,128]{1,0:T(8,128)} %constant.129.clone) | copy-start | bytes 983044
  164.7 2.6 %collective-permute-start.2 = (f32[64,128]{1,0:T(8,128)S(1)}, f32[64,128]{1,0:T(8,128)S(1)}, u32[]{:S(2)}, u32[]{:S(2)}) collective-permute-start(f32[64,128]{1,0:T(8,128)S(1)} %get-tuple-element.32), channel_id=1, source_target_pairs={{0,1},{2,3},{4,5},{6,7},{8,9},{10,11},{12,13},{14,15},{16,17},{18,... | collective-permute-start | bytes 98312 | tf_op jit(solution)/shard_map/ppermute | solution.py:138
  166.1 3.1 %collective-permute-start.3 = (f32[64,128]{1,0:T(8,128)S(1)}, f32[64,128]{1,0:T(8,128)S(1)}, u32[]{:S(2)}, u32[]{:S(2)}) collective-permute-start(f32[64,128]{1,0:T(8,128)S(1)} %get-tuple-element.31), channel_id=1, source_target_pairs={{1,0},{3,2},{5,4},{7,6},{9,8},{11,10},{13,12},{15,14},{17,16},{19,... | collective-permute-start | bytes 98312 | tf_op jit(solution)/shard_map/ppermute | solution.py:139
  167.4 1.8 %copy-start.7 = (f32[512,128]{1,0:T(8,128)}, f32[512,128]{1,0:T(8,128)S(1)}, u32[]{:S(2)}) copy-start(f32[512,128]{1,0:T(8,128)S(1)} %fusion.195) | copy-start | bytes 786436
Sparse Core Ops, SparseCore 0:
  34.3 42.0 all-gather.2
  93.6 69.4 all-reduce.1
